TPU v7x, 256 devices: a whole 4x4x8 slice. The times are simulated.
256 devices in a mesh: seq: 64 (over z, y, core), head: 4 (over x).
Axes of the slice: x: 4, y: 4, z: 8, core: 2. Of those that a mesh axis runs over, the one named last changes fastest.
Arguments:
- queries: bfloat16 [16384, 8192], P('seq', 'head'), may hold values from -6 to 6
- keys: bfloat16 [16384, 8192], P('seq', 'head'), may hold values from -6 to 6
- values: bfloat16 [16384, 8192], P('seq', 'head'), may hold values from -20 to 20
- out_grad: bfloat16 [16384, 8192], P('seq', 'head'), may hold values from -6 to 6
- norm_gain: bfloat16 [8192], P('head'), may hold values from 0.099609375 to 1.8984375
Outputs:
- query_grad: bfloat16 [16384, 8192], P('seq', 'head')
- key_grad: bfloat16 [16384, 8192], P('seq', 'head')
- value_grad: bfloat16 [16384, 8192], P('seq', 'head')
All inputs are finite; a program needn't handle non-finite values.
Results may differ from a plain program's by a relative error of at most 0.0058.
Values sent between devices are 32-bit elements; how exact they have to be, the bound alone decides.
A program may use at most 192 MiB of HBM per device.

v0:
```python
import jax
import jax.numpy as jnp
from jax import lax
from jax.sharding import PartitionSpec as P

DH = 128
GROUP = 256


def carried_in(part, axis, combine, identity, reverse):
    count = lax.axis_size(axis)
    place = lax.axis_index(axis)
    ahead = count - 1 - place if reverse else place
    gathered = lax.all_gather(part, axis)
    state = jnp.zeros_like(part) + jnp.asarray(identity, part.dtype)

    def one(turn, state):
        source = count - 1 - turn if reverse else turn
        return combine(state, lax.dynamic_index_in_dim(gathered, source, 0, False))

    return lax.fori_loop(0, ahead, one, state)


def add_terms(earlier, later):
    return earlier + later


def causal_mask(count):
    rows = lax.broadcasted_iota(jnp.int32, (count, count), 0)
    cols = lax.broadcasted_iota(jnp.int32, (count, count), 1)
    return (rows >= cols).astype(jnp.float32)


def shards(queries, keys, values, out_grad, norm_gain):
    tokens, width = queries.shape
    blocks = tokens // GROUP
    heads = width // DH
    f32 = jnp.float32
    bf16 = jnp.bfloat16

    def to_heads(array):
        return jnp.transpose(array.reshape(blocks, GROUP, heads, DH), (2, 0, 1, 3))

    def to_rows(array):
        return jnp.transpose(array, (1, 2, 0, 3)).reshape(tokens, width)

    query_h, key_h, value_h = (to_heads(queries), to_heads(keys), to_heads(values))
    grad_h = to_heads(out_grad)
    masking = causal_mask(GROUP)
    block_states = jnp.einsum("hncd,hnce->hnde", key_h, value_h, preferred_element_type=f32)
    device_state = jnp.sum(block_states, axis=1)
    earlier = carried_in(device_state, "seq", add_terms, jnp.zeros_like(device_state), False)
    prior = earlier[:, None] + jnp.cumsum(block_states, axis=1) - block_states
    prior_bf = prior.astype(bf16)
    scores = jnp.einsum("hncd,hnkd->hnck", query_h, key_h, preferred_element_type=f32)
    masked = (scores * masking).astype(bf16)
    attn = jnp.einsum("hnck,hnkd->hncd", masked, value_h, preferred_element_type=f32)
    attn = attn + jnp.einsum("hncd,hnde->hnce", query_h, prior_bf, preferred_element_type=f32)
    gain_h = norm_gain.astype(f32).reshape(heads, 1, 1, DH)
    scaled = gain_h * grad_h.astype(f32)
    square_part = jnp.sum(attn * attn, axis=(0, 3))
    cross_part = jnp.sum(scaled * attn, axis=(0, 3))
    square_sum, cross_sum = lax.psum((square_part, cross_part), "head")
    features = lax.axis_size("head") * width
    inverse = lax.rsqrt(square_sum / features + 1e-05)[None, :, :, None]
    cross = (cross_sum / features)[None, :, :, None]
    delta = (inverse * scaled - attn * inverse * inverse * inverse * cross).astype(bf16)
    dscore = jnp.einsum("hnce,hnke->hnck", delta, value_h, preferred_element_type=f32)
    dscore = (dscore * masking).astype(bf16)
    query_grad = jnp.einsum("hnck,hnkd->hncd", dscore, key_h, preferred_element_type=f32)
    query_grad = query_grad + jnp.einsum(
        "hnce,hnde->hncd", delta, prior_bf, preferred_element_type=f32
    )
    grad_states = jnp.einsum("hncd,hnce->hnde", query_h, delta, preferred_element_type=f32)
    grad_device = jnp.sum(grad_states, axis=1)
    after = carried_in(grad_device, "seq", add_terms, jnp.zeros_like(grad_device), True)
    later = after[:, None] + grad_device[:, None] - jnp.cumsum(grad_states, axis=1)
    later_bf = later.astype(bf16)
    key_grad = jnp.einsum("hnck,hncd->hnkd", dscore, query_h, preferred_element_type=f32)
    key_grad = key_grad + jnp.einsum(
        "hnce,hnde->hncd", value_h, later_bf, preferred_element_type=f32
    )
    value_grad = jnp.einsum("hnck,hnce->hnke", masked, delta, preferred_element_type=f32)
    value_grad = value_grad + jnp.einsum(
        "hncd,hnde->hnce", key_h, later_bf, preferred_element_type=f32
    )
    return (
        to_rows(query_grad.astype(bf16)),
        to_rows(key_grad.astype(bf16)),
        to_rows(value_grad.astype(bf16)),
    )


def solution(mesh):
    return jax.shard_map(
        shards,
        mesh=mesh,
        in_specs=(
            P("seq", "head"),
            P("seq", "head"),
            P("seq", "head"),
            P("seq", "head"),
            P("head"),
        ),
        out_specs=(P("seq", "head"), P("seq", "head"), P("seq", "head")),
        check_vma=False,
    )
```

profile of v0, /device:TPU:1, one launch (start us, length us, event | category | flops | bytes accessed | tf_op | source)
XLA Modules:
  0.0 711.3 jit_solution(11280510497541795035)
XLA Ops:
  7.2 1.5 copy.59
  10.1 1.6 fusion.13
  13.2 2.6 copy.31
  18.1 2.2 fusion.18
  20.3 232.1 %all-gather.5.cloned.1.call-done = f32[1024,128,128]{2,1,0:T(8,128)} async-done(((f32[16,128,128]{2,1,0:T(8,128)}), f32[1024,128,128]{2,1,0:T(8,128)}) %all-gather.5.cloned.1.call-update) | async-done | bytes 67108880 | tf_op jit(solution)/shard_map/all_gather | solution.py:14
  252.5 1.5 while.22
  252.5 1.5 bitcast_add_fusion.7
  254.0 1.5 fusion.4
  255.9 2.4 fusion.3
  259.9 8.4 %all-reduce = (f32[1,256]{1,0:T(1,128)S(1)}, f32[1,256]{1,0:T(1,128)S(1)}) all-reduce(f32[1,256]{1,0:T(1,128)S(1)} %bitcast.145, f32[1,256]{1,0:T(1,128)S(1)} %bitcast.146), channel_id=1, replica_groups=mesh['seq'=64,'head'=4] {'head'}, use_global_device_ids=true, to_apply=%region_5.6 | all-reduce | flops 512 | bytes 4096 | tf_op jit(solution)/shard_map/psum | solution.py:63
  268.3 2.8 fusion.6
  271.1 1.5 convolution_bitcast_fusion
  272.6 2.6 copy.36
  280.9 3.5 fusion.32
  284.4 1.9 fusion.7
  286.3 312.2 %all-gather.7.cloned.1.call-done = f32[1024,128,128]{2,1,0:T(8,128)} async-done(((f32[16,128,128]{2,1,0:T(8,128)}), f32[1024,128,128]{2,1,0:T(8,128)}) %all-gather.7.cloned.1.call-update) | async-done | bytes 67108880 | tf_op jit(solution)/shard_map/all_gather | solution.py:14
  598.6 93.7 %while.23 = (s32[]{:T(128)}, f32[16,128,128]{2,1,0:T(8,128)S(1)}, s32[]{:T(128)}, f32[64,16,128,128]{3,2,1,0:T(8,128)}, s32[]{:T(128)}, /*index=5*/s32[]{:T(128)}, s32[]{:T(128)}, s32[]{:T(128)}) while((s32[]{:T(128)}, f32[16,128,128]{2,1,0:T(8,128)S(1)}, s32[]{:T(128)}, f32[64,16,128,128]{3,2,1,0:T(8,128)}, s32[]{:T(128)}, ...), condition=%wide.region_7.8_spmd, body=%wide.region_6.7_spmd.sunk | while | flops 262150 | bytes 3145871 | solution.py:21
  598.6 1.5 bitcast_add_fusion.8
  600.1 1.5 bitcast_add_fusion.8
  601.6 1.5 bitcast_add_fusion.8
  603.2 1.5 bitcast_add_fusion.8
  604.7 1.5 bitcast_add_fusion.8
  606.2 1.5 bitcast_add_fusion.8
  607.7 1.5 bitcast_add_fusion.8
  609.2 1.5 bitcast_add_fusion.8
  631.9 1.5 bitcast_add_fusion.8
  660.6 1.5 bitcast_add_fusion.8
  689.3 1.5 bitcast_add_fusion.8
  693.6 1.8 fusion.5
  697.3 2.4 copy.41
  699.7 2.5 fusion.1
  702.2 2.3 copy.40
  (107 shorter events, 92.0 us)
Async XLA Ops:
  7.2 245.2 %all-gather.5.cloned.1.call-start = ((), (), s32[]{:S(2)}) async-start(), calls=%async_computation | async-start | bytes 68157440 | tf_op jit(solution)/shard_map/all_gather | solution.py:14
  7.2 1.8 copy-start.15
  8.8 7.3 %copy-start.5 = (bf16[32,8,16,128]{3,2,1,0:T(8,128)(2,1)}, bf16[32,8,16,128]{3,2,1,0:T(8,128)(2,1)S(1)}, u32[]{:S(2)}) copy-start(bf16[32,8,16,128]{3,2,1,0:T(8,128)(2,1)S(1)} %copy.59) | copy-start | bytes 3145732
  9.0 1.1 copy-start.7
  11.7 586.8 %all-gather.7.cloned.1.call-start = ((), (), s32[]{:S(2)}) async-start(), calls=%async_computation.1 | async-start | bytes 68157440 | tf_op jit(solution)/shard_map/all_gather | solution.py:14
  13.2 2.6 copy-start.16
  16.8 1.4 copy-start
  254.0 1.9 copy-start.1
  255.5 2.8 copy-start.11
  258.3 1.3 copy-start.2
  276.4 1.2 copy-start.8
  277.6 1.3 copy-start.3
  277.6 1.4 copy-start.12
  280.9 3.5 copy-start.4
  280.9 3.5 copy-start.14
  692.3 3.2 copy-start.6
  693.6 2.2 copy-start.10
  695.8 1.5 copy-start.13
  697.3 2.4 copy-start.9
Sparse Core Ops, SparseCore 0:
  11.8 240.5 all-gather.4
  275.3 323.1 all-gather.6
where the time goes:
time: 714 us; the launch traced here: 711 us
  waiting for transfers between devices  544 us (76%)
  other arithmetic  100 us (14%)
  local copies, waits for them, and re-layouts  22.9 us (3%)
  matrix products  19.8 us (3%)
  between operations  14.3 us (2%)
  blocking collectives  8.39 us (1%)
    all_gather x2, waiting for transfers between devices, carried_in(): gathered = lax.all_gather(part, axis)  544 us
    add x63, other arithmetic, add_terms(): return earlier + later  93.8 us
    unnamed x40, local copies, waits for them, and re-layouts  14.7 us
  transfers between devices with their start and end apart: 2, of which 2 were waited for; matrix products, arithmetic and copies ran while one was open for 2% of the time, Pallas kernels for 0%

commit v1 on v0

v1 whole, which is shorter than its diff:
```python
import jax
import jax.numpy as jnp
from jax import lax
from jax.experimental import pallas as pl
from jax.experimental.pallas import tpu as pltpu
from jax.sharding import PartitionSpec as P

DH = 128
GROUP = 256
HEADS = 16
HALF = 8
NZ = 8
NY = 4
CHIPS = NZ * NY
NX = 4
ROWS = HALF * DH // CHIPS
SPLIT = DH // ROWS
MESH = pl.DeviceIdType.MESH
FAR_Z = (4, 3, 5, 2, 6, 1, 7, 0)
FAR_Y = (2, 1, 3, 0)
OFFSETS = [(dz, dy) for dz in FAR_Z for dy in FAR_Y if (dz, dy) != (0, 0)]

f32 = jnp.float32
bf16 = jnp.bfloat16


def dot(a, b, dim_a, dim_b):
    return lax.dot_general(
        a, b, (((dim_a,), (dim_b,)), ((), ())), preferred_element_type=f32
    )


def kernel(
    q_hbm, k_hbm, v_hbm, g_hbm, gain_ref,
    qg_hbm, kg_hbm, vg_hbm,
    q, k, v, g, attn, delta, scores, dscore, qg, kg, vg, state,
    own, swap, chip, gather, parts, back, ahead, arrived,
    norm_send, norm_got,
    in_sem, out_sem, swap_sem, out_a2a_sem, back_send_sem, back_sem, ahead_sem, norm_sem,
):
    seq = lax.axis_index("seq")
    plane = lax.axis_index("head")
    core = lax.rem(seq, 2)
    here = seq // 2
    z, y = here // NY, lax.rem(here, NY)
    other = (seq + 1 - 2 * core, plane)

    def chip_at(dz, dy):
        return lax.rem(z + dz, NZ) * NY + lax.rem(y + dy, NY)

    def device_of(place):
        return (place * 2 + core, plane)

    def across(step):
        return (seq, lax.rem(plane + step, NX))

    loads = [
        pltpu.make_async_copy(src, dst, in_sem.at[i])
        for i, (src, dst) in enumerate(((k_hbm, k), (v_hbm, v), (q_hbm, q), (g_hbm, g)))
    ]
    for load in loads:
        load.start()

    barrier = pltpu.get_barrier_semaphore()
    pl.semaphore_signal(barrier, inc=1, device_id=other, device_id_type=MESH)
    for dz, dy in OFFSETS:
        pl.semaphore_signal(
            barrier, inc=1, device_id=device_of(chip_at(dz, dy)), device_id_type=MESH
        )
    for step in range(1, NX):
        pl.semaphore_signal(barrier, inc=1, device_id=across(step), device_id_type=MESH)

    mine = core * HALF
    theirs = HALF - mine

    def cols(head):
        return pl.ds(pl.multiple_of(head * DH, DH), DH)

    def each(first, body):
        def one(i, carry):
            body(i, first + i)
            return carry

        lax.fori_loop(0, HALF, one, 0)

    def swap_half(s, term, first):
        def fill(half):
            def body(i, head):
                own[s, half, pl.ds(i * SPLIT, SPLIT)] = term(head).reshape(SPLIT, ROWS, DH)

            return body

        each(theirs, fill(1 - core))
        if first:
            pl.semaphore_wait(barrier, 1 + len(OFFSETS) + NX - 1)
        copy = pltpu.make_async_remote_copy(
            src_ref=own.at[s, 1 - core],
            dst_ref=swap.at[s],
            send_sem=swap_sem.at[s, 0],
            recv_sem=swap_sem.at[s, 1],
            device_id=other,
            device_id_type=MESH,
        )
        copy.start()
        each(mine, fill(core))
        copy.wait()
        chip[s] = own[s, core] + swap[s]

    def spread(s):
        for dz, dy in OFFSETS:
            place = chip_at(dz, dy)
            pltpu.make_async_remote_copy(
                src_ref=chip.at[s, place],
                dst_ref=gather.at[s, here],
                send_sem=out_a2a_sem.at[s, 0],
                recv_sem=out_a2a_sem.at[s, 1],
                device_id=device_of(place),
                device_id_type=MESH,
            ).start()
        gather[s, here] = chip[s, here]

    def wait_for(ref, sem):
        pltpu.make_async_copy(ref, ref, sem).wait()

    def sum_up(s, reverse):
        wait_for(gather.at[s, pl.ds(0, CHIPS - 1)], out_a2a_sem.at[s, 1])
        total = jnp.zeros((ROWS, DH), f32)
        for place in range(CHIPS - 1, -1, -1) if reverse else range(CHIPS):
            parts[s, place] = total
            total = total + gather[s, place]

    def send_back(s):
        for dz, dy in OFFSETS:
            place = chip_at(dz, dy)
            pltpu.make_async_remote_copy(
                src_ref=parts.at[s, place],
                dst_ref=back.at[s, here],
                send_sem=back_send_sem.at[s],
                recv_sem=back_sem.at[s, here // SPLIT],
                device_id=device_of(place),
                device_id_type=MESH,
            ).start()
        pltpu.make_async_copy(
            parts.at[s, here], back.at[s, here], back_sem.at[s, here // SPLIT]
        ).start()

    def ahead_copy(s, i):
        return pltpu.make_async_remote_copy(
            src_ref=ahead.at[s, i],
            dst_ref=arrived.at[s, i],
            send_sem=ahead_sem.at[s, 0, i],
            recv_sem=ahead_sem.at[s, 1, i],
            device_id=other,
            device_id_type=MESH,
        )

    def collect(s, inner, use):
        def mine_one(i, head):
            rows = pl.ds(i * SPLIT, SPLIT)
            wait_for(back.at[s, rows], back_sem.at[s, i])
            chip_part = back[s, rows].reshape(DH, DH)
            here_is_inner = core == inner
            extra = jnp.where(here_is_inner, own[s, core, rows], swap[s, rows]).reshape(DH, DH)
            both = chip_part + extra
            ahead[s, i] = jnp.where(here_is_inner, both, chip_part)
            ahead_copy(s, i).start()
            use(head, jnp.where(here_is_inner, chip_part, both).astype(bf16))

        each(mine, mine_one)

        def theirs_one(i, head):
            ahead_copy(s, i).wait_recv()
            use(head, arrived[s, i].astype(bf16))

        each(theirs, theirs_one)

    def finish_sends(s):
        sent = pl.ds(0, CHIPS - 1)
        wait_for(chip.at[s, sent], out_a2a_sem.at[s, 0])
        wait_for(parts.at[s, sent], back_send_sem.at[s])
        each(0, lambda i, head: ahead_copy(s, i).wait_send())

    rows = lax.broadcasted_iota(jnp.int32, (GROUP, GROUP), 0)
    columns = lax.broadcasted_iota(jnp.int32, (GROUP, GROUP), 1)
    causal = rows >= columns

    loads[0].wait()
    loads[1].wait()
    swap_half(0, lambda head: dot(k[:, cols(head)], v[:, cols(head)], 0, 0), True)
    spread(0)
    loads[2].wait()
    loads[3].wait()

    def within(i, head):
        at = cols(head)
        part = dot(q[:, at], k[:, at], 1, 1)
        masked = jnp.where(causal, part, 0.0).astype(bf16)
        scores[head] = masked
        attn[:, at] = dot(masked, v[:, at], 1, 0)

    each(0, within)
    sum_up(0, False)
    send_back(0)
    each(HALF, within)

    squares = norm_send.at[0]
    crosses = norm_send.at[1]
    squares[...] = jnp.zeros_like(squares)
    crosses[...] = jnp.zeros_like(crosses)

    def finish_attn(head, state_b):
        at = cols(head)
        state[head] = state_b
        value = attn[:, at] + dot(q[:, at], state_b, 1, 0)
        attn[:, at] = value
        squares[...] += value * value
        crosses[...] += gain_ref[:, at].astype(f32) * g[:, at].astype(f32) * value

    collect(0, 0, finish_attn)

    norm_got[plane, 0:1] = jnp.sum(squares[...].T, axis=0, keepdims=True)
    norm_got[plane, 1:2] = jnp.sum(crosses[...].T, axis=0, keepdims=True)
    for step in range(1, NX):
        pltpu.make_async_remote_copy(
            src_ref=norm_got.at[plane],
            dst_ref=norm_got.at[plane],
            send_sem=norm_sem.at[0],
            recv_sem=norm_sem.at[1],
            device_id=across(step),
            device_id_type=MESH,
        ).start()
    wait_for(norm_got.at[pl.ds(0, NX - 1)], norm_sem.at[1])
    sums = norm_got[0] + norm_got[1] + norm_got[2] + norm_got[3]
    features = float(NX * HEADS * DH)
    inverse = lax.rsqrt(sums[0:1] / features + 1e-05)
    weight = inverse * inverse * inverse * (sums[1:2] / features)
    wait_for(norm_got.at[pl.ds(0, NX - 1)], norm_sem.at[0])
    squares[...] = jnp.broadcast_to(inverse, (DH, GROUP)).T
    crosses[...] = jnp.broadcast_to(weight, (DH, GROUP)).T

    def outer(head):
        at = cols(head)
        scaled = gain_ref[:, at].astype(f32) * g[:, at].astype(f32)
        value = (squares[...] * scaled - attn[:, at] * crosses[...]).astype(bf16)
        delta[:, at] = value
        return dot(q[:, at], value, 0, 0)

    swap_half(1, outer, False)
    spread(1)

    def query_side(i, head):
        at = cols(head)
        part = dot(delta[:, at], v[:, at], 1, 1)
        masked = jnp.where(causal, part, 0.0).astype(bf16)
        dscore[head] = masked
        grad = dot(masked, k[:, at], 1, 0) + dot(delta[:, at], state[head], 1, 1)
        qg[:, at] = grad.astype(bf16)

    each(0, query_side)
    each(HALF, query_side)
    qg_out = pltpu.make_async_copy(qg, qg_hbm, out_sem.at[0])
    qg_out.start()
    sum_up(1, True)
    send_back(1)

    def key_side(i, head):
        at = cols(head)
        kg[:, at] = dot(dscore[head], q[:, at], 0, 0)
        vg[:, at] = dot(scores[head], delta[:, at], 0, 0)

    each(0, key_side)
    each(HALF, key_side)

    def finish_keys(head, later_b):
        at = cols(head)
        k_grad = kg[:, at] + dot(v[:, at], later_b, 1, 1)
        v_grad = vg[:, at] + dot(k[:, at], later_b, 1, 0)
        q[:, at] = k_grad.astype(bf16)
        g[:, at] = v_grad.astype(bf16)

    collect(1, 1, finish_keys)
    kg_out = pltpu.make_async_copy(q, kg_hbm, out_sem.at[1])
    vg_out = pltpu.make_async_copy(g, vg_hbm, out_sem.at[2])
    kg_out.start()
    vg_out.start()
    finish_sends(0)
    finish_sends(1)
    qg_out.wait()
    kg_out.wait()
    vg_out.wait()


def shards(queries, keys, values, out_grad, norm_gain):
    tokens, width = queries.shape
    vmem = pltpu.VMEM
    grad = jax.ShapeDtypeStruct((tokens, width), bf16)
    hbm = pl.BlockSpec(memory_space=pl.ANY)
    slices = (2, CHIPS, ROWS, DH)
    halves = (2, 2, CHIPS, ROWS, DH)
    dma = pltpu.SemaphoreType.DMA
    return pl.pallas_call(
        kernel,
        out_shape=(grad, grad, grad),
        in_specs=[hbm, hbm, hbm, hbm, pl.BlockSpec(memory_space=pltpu.VMEM)],
        out_specs=(hbm, hbm, hbm),
        scratch_shapes=[
            vmem((tokens, width), bf16),
            vmem((tokens, width), bf16),
            vmem((tokens, width), bf16),
            vmem((tokens, width), bf16),
            vmem((tokens, width), f32),
            vmem((tokens, width), bf16),
            vmem((HEADS, GROUP, GROUP), bf16),
            vmem((HEADS, GROUP, GROUP), bf16),
            vmem((tokens, width), bf16),
            vmem((tokens, width), f32),
            vmem((tokens, width), f32),
            vmem((HEADS, DH, DH), bf16),
            vmem(halves, f32),
            vmem(slices, f32),
            vmem(slices, f32),
            vmem(slices, f32),
            vmem(slices, f32),
            vmem(slices, f32),
            vmem((2, HALF, DH, DH), f32),
            vmem((2, HALF, DH, DH), f32),
            vmem((2, GROUP, DH), f32),
            vmem((NX, 8, GROUP), f32),
            dma((4,)),
            dma((3,)),
            dma((2, 2)),
            dma((2, 2)),
            dma((2,)),
            dma((2, HALF)),
            dma((2, 2, HALF)),
            dma((2,)),
        ],
        compiler_params=pltpu.CompilerParams(
            collective_id=0, has_side_effects=True, vmem_limit_bytes=56 * 2**20
        ),
        name="block_backward",
    )(queries, keys, values, out_grad, norm_gain.reshape(1, width))


def solution(mesh):
    return jax.shard_map(
        shards,
        mesh=mesh,
        in_specs=(
            P("seq", "head"),
            P("seq", "head"),
            P("seq", "head"),
            P("seq", "head"),
            P("head"),
        ),
        out_specs=(P("seq", "head"), P("seq", "head"), P("seq", "head")),
        check_vma=False,
    )
```

time: 714 us -> 91.7 us (0.13)
  waiting for transfers between devices: 544 us -> 0 us
  other arithmetic: 100 us -> 0 us
  Pallas kernels: 0 us -> 84.6 us
  matrix products: 19.8 us -> 0 us
  local copies, waits for them, and re-layouts: 22.9 us -> 6.26 us
  between operations: 14.3 us -> 0.65 us
  blocking collectives: 8.39 us -> 0 us
    all_gather x2 -> x0, waiting for transfers between devices: 544 us -> none  [carried_in(): gathered = lax.all_gather(part, axis)]
    add x63 -> x0, other arithmetic: 93.8 us -> none  [add_terms(): return earlier + later]
    pallas_call x0 -> x1, Pallas kernels: none -> 84.6 us  [shards(): pl.pallas_call(kernel, out_shape=(grad, grad, grad), in_specs=[hbm, hbm,...]
    dot_general x12 -> x0, matrix products: 19.8 us -> none  [the longest x1 3.54 us: shards(): jnp.einsum('hnck,hnce->hnke', masked, delta, preferred_element_type=f32)]
    unnamed x40 -> x7, local copies, waits for them, and re-layouts: 14.7 us -> 4.97 us
    psum x1 -> x0, blocking collectives: 8.39 us -> none  [shards(): square_sum, cross_sum = lax.psum((square_part, cross_part), 'head')]
  transfers between devices with their start and end apart: 2 -> 0, of which waited for: 2 -> 0; matrix products, arithmetic and copies ran while one was open for 2% -> 0% of each run, Pallas kernels for 0% -> 0%
where the time goes in v1:
time: 91.7 us; the launch traced here: 91.5 us
  Pallas kernels  84.6 us (92%)
  local copies, waits for them, and re-layouts  6.26 us (7%)
    pallas_call x1, Pallas kernels, shards(): pl.pallas_call(kernel, out_shape=(grad, grad, grad), in_specs=[hbm, hbm,...  84.6 us
    unnamed x7, local copies, waits for them, and re-layouts  4.97 us

profile of v1, /device:TPU:1, one launch (start us, length us, event | category | flops | bytes accessed | tf_op | source)
XLA Modules:
  0.0 91.5 jit_solution(223218745379538498)
XLA Ops:
  0.6 1.3 %reshape.9.gain_ref = bf16[1,2048]{1,0:T(2,128)(2,1)} reshape(bf16[2048]{0:T(1024)(128)(2,1)} %param.9) | data formatting | bytes 8192 | tf_op jit(solution)/shard_map/reshape | solution.py:342
  1.9 84.6 %block_backward.1 = (bf16[256,2048]{1,0:T(8,128)(2,1)}, bf16[256,2048]{1,0:T(8,128)(2,1)}, bf16[256,2048]{1,0:T(8,128)(2,1)}) custom-call(bf16[256,2048]{1,0:T(8,128)(2,1)} %q_hbm.1, bf16[256,2048]{1,0:T(8,128)(2,1)} %k_hbm.1, bf16[256,2048]{1,0:T(8,128)(2,1)} %v_hbm.1, bf16[256,2048]{1,0:T(8,128)(2,1)} %g_hbm.1, bf16[1,2048]{1,0:T(2,128)(2,1)} %reshape.9.gain_ref), custom_call_target="tpu_custom_call" | custom-call | tf_op jit(solution)/shard_map/block_backward/pallas_call | solution.py:301
  86.5 0.0 copy-start.1
  86.5 2.4 %copy.11 = bf16[256,2048]{1,0:T(8,128)(2,1)} copy(bf16[256,2048]{1,0:T(8,128)(2,1)} %get-tuple-element.6) | data formatting | bytes 2097152
  88.9 0.0 copy-done.1
  88.9 0.0 copy-start
  88.9 1.0 %copy.12 = bf16[256,2048]{1,0:T(8,128)(2,1)} copy(bf16[256,2048]{1,0:T(8,128)(2,1)S(1)} %copy-done.1) | data formatting | bytes 2097152
  89.9 0.6 copy-done
  90.5 1.0 %copy.13 = bf16[256,2048]{1,0:T(8,128)(2,1)} copy(bf16[256,2048]{1,0:T(8,128)(2,1)S(1)} %copy-done) | data formatting | bytes 2097152
Async XLA Ops:
  86.5 2.4 %copy-start.1 = (bf16[256,2048]{1,0:T(8,128)(2,1)S(1)}, bf16[256,2048]{1,0:T(8,128)(2,1)}, u32[]{:S(2)}) copy-start(bf16[256,2048]{1,0:T(8,128)(2,1)} %get-tuple-element.7) | copy-start | bytes 3145732
  88.9 1.6 %copy-start = (bf16[256,2048]{1,0:T(8,128)(2,1)S(1)}, bf16[256,2048]{1,0:T(8,128)(2,1)}, u32[]{:S(2)}) copy-start(bf16[256,2048]{1,0:T(8,128)(2,1)} %get-tuple-element.8) | copy-start | bytes 3145732

commit v2 on v0

v2 whole, which is shorter than its diff:
```python
import jax
import jax.numpy as jnp
from jax import lax
from jax.experimental import pallas as pl
from jax.experimental.pallas import tpu as pltpu
from jax.sharding import PartitionSpec as P

DH = 128
GROUP = 256
HEADS = 16
HALF = 8
NZ = 8
NY = 4
NX = 4
CHUNKS = 4
PER = HALF // CHUNKS
YROWS = PER * DH // NY
ZROWS = YROWS // NZ
MESH = pl.DeviceIdType.MESH
FAR_Z = (4, 3, 5, 2, 6, 1, 7)
FAR_Y = (2, 1, 3)
PEERS = 1 + len(FAR_Z) + len(FAR_Y) + NX - 1

f32 = jnp.float32
bf16 = jnp.bfloat16


def dot(a, b, dim_a, dim_b):
    return lax.dot_general(
        a, b, (((dim_a,), (dim_b,)), ((), ())), preferred_element_type=f32
    )


def wait_for(ref, sem):
    pltpu.make_async_copy(ref, ref, sem).wait()


def kernel(
    q_hbm, k_hbm, v_hbm, g_hbm, gain_hbm,
    qg, kg, vg,
    q, k, v, g, gain, q_t, attn, scaled, delta, scores, dscore, kg_part, vg_part, state,
    own, swap, chip, y_got, y_sum, z_got, z_part, z_back, y_part, y_back, ahead, arrived,
    norm_acc, norm_got,
    in_sem, swap_sem, y_sem, z_sem, zb_sem, yb_sem, ahead_sem, norm_sem,
):
    seq = lax.axis_index("seq")
    plane = lax.axis_index("head")
    core = lax.rem(seq, 2)
    z, y = seq // (2 * NY), lax.rem(seq // 2, NY)
    other = (seq + 1 - 2 * core, plane)
    y_peers = [lax.rem(y + step, NY) for step in FAR_Y]
    z_peers = [lax.rem(z + step, NZ) for step in FAR_Z]

    def at_y(place):
        return ((z * NY + place) * 2 + core, plane)

    def at_z(place):
        return ((place * NY + y) * 2 + core, plane)

    def across(step):
        return (seq, lax.rem(plane + step, NX))

    loads = [
        pltpu.make_async_copy(src, dst, in_sem.at[i])
        for i, (src, dst) in enumerate(
            ((k_hbm, k), (v_hbm, v), (q_hbm, q), (g_hbm, g), (gain_hbm, gain))
        )
    ]
    for load in loads:
        load.start()

    barrier = pltpu.get_barrier_semaphore()
    for place in z_peers:
        pl.semaphore_signal(barrier, inc=1, device_id=at_z(place), device_id_type=MESH)
    for place in y_peers:
        pl.semaphore_signal(barrier, inc=1, device_id=at_y(place), device_id_type=MESH)
    for step in range(1, NX):
        pl.semaphore_signal(barrier, inc=1, device_id=across(step), device_id_type=MESH)
    pl.semaphore_signal(barrier, inc=1, device_id=other, device_id_type=MESH)

    mine = core * HALF
    theirs = HALF - mine

    def cols(head):
        return pl.ds(pl.multiple_of(head * DH, DH), DH)

    def send(src, dst, sem, device):
        pltpu.make_async_remote_copy(
            src_ref=src,
            dst_ref=dst,
            send_sem=sem.at[0],
            recv_sem=sem.at[1],
            device_id=device,
            device_id_type=MESH,
        ).start()

    def swap_out(s, c, term):
        for j in range(PER):
            own[s, 1 - core, c, pl.ds(j * DH, DH)] = term(theirs + c * PER + j)
        send(own.at[s, 1 - core, c], swap.at[s, c], swap_sem.at[s, c], other)

    def y_out(s, c, term):
        for j in range(PER):
            own[s, core, c, pl.ds(j * DH, DH)] = term(mine + c * PER + j)
        wait_for(swap.at[s, c], swap_sem.at[s, c, 1])
        chip[s, c] = (own[s, core, c] + swap[s, c]).reshape(NY, YROWS, DH)
        for place in y_peers:
            send(chip.at[s, c, place], y_got.at[s, c, y], y_sem.at[s, c], at_y(place))
        y_got[s, c, y] = chip[s, c, y]

    def z_out(s, c):
        wait_for(y_got.at[s, c, pl.ds(0, NY - 1)], y_sem.at[s, c, 1])
        total = (y_got[s, c, 0] + y_got[s, c, 1]) + (y_got[s, c, 2] + y_got[s, c, 3])
        y_sum[s, c] = total.reshape(NZ, ZROWS, DH)
        for place in z_peers:
            send(y_sum.at[s, c, place], z_got.at[s, c, z], z_sem.at[s, c], at_z(place))
        z_got[s, c, z] = y_sum[s, c, z]

    def z_return(s, c, reverse):
        wait_for(z_got.at[s, c, pl.ds(0, NZ - 1)], z_sem.at[s, c, 1])
        total = jnp.zeros((ZROWS, DH), f32)
        for place in range(NZ - 1, -1, -1) if reverse else range(NZ):
            z_part[s, c, place] = total
            total = total + z_got[s, c, place]
        for place in z_peers:
            send(z_part.at[s, c, place], z_back.at[s, c, z], zb_sem.at[s, c], at_z(place))
        z_back[s, c, z] = z_part[s, c, z]

    def y_return(s, c, reverse):
        wait_for(z_back.at[s, c, pl.ds(0, NZ - 1)], zb_sem.at[s, c, 1])
        total = z_back[s, c].reshape(YROWS, DH)
        for place in range(NY - 1, -1, -1) if reverse else range(NY):
            y_part[s, c, place] = total
            total = total + y_got[s, c, place]
        for place in y_peers:
            send(y_part.at[s, c, place], y_back.at[s, c, y], yb_sem.at[s, c], at_y(place))
        y_back[s, c, y] = y_part[s, c, y]

    def collect(s, c, inner, use):
        wait_for(y_back.at[s, c, pl.ds(0, NY - 1)], yb_sem.at[s, c, 1])
        chip_part = y_back[s, c].reshape(PER * DH, DH)
        is_inner = core == inner
        both = chip_part + jnp.where(is_inner, own[s, core, c], swap[s, c])
        ahead[s, c] = jnp.where(is_inner, both, chip_part)
        send(ahead.at[s, c], arrived.at[s, c], ahead_sem.at[s, c], other)
        result = jnp.where(is_inner, chip_part, both).astype(bf16)
        for j in range(PER):
            use(mine + c * PER + j, result[j * DH:(j + 1) * DH])

    def collect_theirs(s, c, use):
        wait_for(arrived.at[s, c], ahead_sem.at[s, c, 1])
        result = arrived[s, c].astype(bf16)
        for j in range(PER):
            use(theirs + c * PER + j, result[j * DH:(j + 1) * DH])

    def finish_sends(s):
        for c in range(CHUNKS):
            wait_for(swap.at[s, c], swap_sem.at[s, c, 0])
            wait_for(y_got.at[s, c, pl.ds(0, NY - 1)], y_sem.at[s, c, 0])
            wait_for(z_got.at[s, c, pl.ds(0, NZ - 1)], z_sem.at[s, c, 0])
            wait_for(z_back.at[s, c, pl.ds(0, NZ - 1)], zb_sem.at[s, c, 0])
            wait_for(y_back.at[s, c, pl.ds(0, NY - 1)], yb_sem.at[s, c, 0])
            wait_for(arrived.at[s, c], ahead_sem.at[s, c, 0])

    def heads(first, count, body):
        def pair(i, carry):
            body(first + 2 * i)
            body(first + 2 * i + 1)
            return carry

        lax.fori_loop(0, count // 2, pair, 0)

    chunks = range(CHUNKS)
    rows = lax.broadcasted_iota(jnp.int32, (GROUP, GROUP), 0)
    columns = lax.broadcasted_iota(jnp.int32, (GROUP, GROUP), 1)
    causal = rows >= columns

    def key_value(head):
        return dot(k[:, cols(head)], v[:, cols(head)], 0, 0)

    loads[0].wait()
    loads[1].wait()
    pl.semaphore_wait(barrier, PEERS)
    for c in chunks:
        swap_out(0, c, key_value)
    for c in chunks:
        y_out(0, c, key_value)
    for load in loads[2:]:
        load.wait()

    def within(head):
        at = cols(head)
        part = dot(q[:, at], k[:, at], 1, 1)
        masked = jnp.where(causal, part, 0.0).astype(bf16)
        scores[head] = masked
        attn[:, at] = dot(masked, v[:, at], 1, 0)

    def prepare(i, carry):
        for head in (2 * i, 2 * i + 1):
            q_t[head] = q[:, cols(head)].T
        at = pl.ds(pl.multiple_of(i * 2 * DH, 2 * DH), 2 * DH)
        scaled[:, at] = gain[at].astype(f32).reshape(1, 2 * DH) * g[:, at].astype(f32)
        return carry

    heads(0, HALF, within)
    for c in chunks:
        z_out(0, c)
    heads(HALF, HALF, within)
    for c in chunks:
        z_return(0, c, False)
    lax.fori_loop(0, HEADS // 2, prepare, 0)
    for c in chunks:
        y_return(0, c, False)
    norm_acc[...] = jnp.zeros_like(norm_acc)

    def finish_attn(head, state_b):
        at = cols(head)
        state[head] = state_b
        value = attn[:, at] + dot(q[:, at], state_b, 1, 0)
        attn[:, at] = value
        norm_acc[0] += value * value
        norm_acc[1] += scaled[:, at] * value

    for c in chunks:
        collect(0, c, 0, finish_attn)
    for c in chunks:
        collect_theirs(0, c, finish_attn)

    norm_got[plane, 0:1] = jnp.sum(norm_acc[0].T, axis=0, keepdims=True)
    norm_got[plane, 1:2] = jnp.sum(norm_acc[1].T, axis=0, keepdims=True)
    for step in (2, 1, 3):
        send(norm_got.at[plane], norm_got.at[plane], norm_sem, across(step))
    wait_for(norm_got.at[pl.ds(0, NX - 1)], norm_sem.at[1])
    sums = (norm_got[0] + norm_got[1]) + (norm_got[2] + norm_got[3])
    features = float(NX * HEADS * DH)
    inverse = lax.rsqrt(sums[0:1] / features + 1e-05)
    weight = inverse * inverse * inverse * (sums[1:2] / features)
    wait_for(norm_got.at[pl.ds(0, NX - 1)], norm_sem.at[0])
    norm_acc[0] = jnp.broadcast_to(inverse, (DH, GROUP)).T
    norm_acc[1] = jnp.broadcast_to(weight, (DH, GROUP)).T

    def query_delta(head):
        at = cols(head)
        value = (norm_acc[0] * scaled[:, at] - attn[:, at] * norm_acc[1]).astype(bf16)
        delta[:, at] = value
        return dot(q_t[head], value, 1, 0)

    for c in chunks:
        swap_out(1, c, query_delta)
    for c in chunks:
        y_out(1, c, query_delta)

    def query_side(head):
        at = cols(head)
        part = dot(delta[:, at], v[:, at], 1, 1)
        masked = jnp.where(causal, part, 0.0).astype(bf16)
        dscore[head] = masked
        grad = dot(masked, k[:, at], 1, 0) + dot(delta[:, at], state[head], 1, 1)
        qg[:, at] = grad.astype(bf16)

    def key_side(head):
        at = cols(head)
        kg_part[:, at] = dot(dscore[head], q[:, at], 0, 0)
        vg_part[:, at] = dot(scores[head], delta[:, at], 0, 0)

    heads(0, HALF, query_side)
    for c in chunks:
        z_out(1, c)
    heads(HALF, HALF, query_side)
    for c in chunks:
        z_return(1, c, True)
    heads(0, HALF, key_side)
    for c in chunks:
        y_return(1, c, True)
    heads(HALF, HALF, key_side)

    def finish_keys(head, later_b):
        at = cols(head)
        kg[:, at] = (kg_part[:, at] + dot(v[:, at], later_b, 1, 1)).astype(bf16)
        vg[:, at] = (vg_part[:, at] + dot(k[:, at], later_b, 1, 0)).astype(bf16)

    for c in chunks:
        collect(1, c, 1, finish_keys)
    for c in chunks:
        collect_theirs(1, c, finish_keys)
    finish_sends(0)
    finish_sends(1)


def shards(queries, keys, values, out_grad, norm_gain):
    tokens, width = queries.shape
    vmem = pltpu.VMEM
    grad = jax.ShapeDtypeStruct((tokens, width), bf16)
    hbm = pl.BlockSpec(memory_space=pltpu.HBM)
    on_chip = pl.BlockSpec(memory_space=pltpu.VMEM)
    dma = pltpu.SemaphoreType.DMA
    flat = (2, CHUNKS, PER * DH, DH)
    by_y = (2, CHUNKS, NY, YROWS, DH)
    by_z = (2, CHUNKS, NZ, ZROWS, DH)
    pairs = (2, CHUNKS, 2)
    return pl.pallas_call(
        kernel,
        out_shape=(grad, grad, grad),
        in_specs=[hbm, hbm, hbm, hbm, hbm],
        out_specs=(on_chip, on_chip, on_chip),
        scratch_shapes=[
            vmem((tokens, width), bf16),
            vmem((tokens, width), bf16),
            vmem((tokens, width), bf16),
            vmem((tokens, width), bf16),
            vmem((width,), bf16),
            vmem((HEADS, DH, GROUP), bf16),
            vmem((tokens, width), f32),
            vmem((tokens, width), f32),
            vmem((tokens, width), bf16),
            vmem((HEADS, GROUP, GROUP), bf16),
            vmem((HEADS, GROUP, GROUP), bf16),
            vmem((tokens, width), f32),
            vmem((tokens, width), f32),
            vmem((HEADS, DH, DH), bf16),
            vmem((2, 2, CHUNKS, PER * DH, DH), f32),
            vmem(flat, f32),
            vmem(by_y, f32),
            vmem(by_y, f32),
            vmem(by_z, f32),
            vmem(by_z, f32),
            vmem(by_z, f32),
            vmem(by_z, f32),
            vmem(by_y, f32),
            vmem(by_y, f32),
            vmem(flat, f32),
            vmem(flat, f32),
            vmem((2, GROUP, DH), f32),
            vmem((NX, 8, GROUP), f32),
            dma((5,)),
            dma(pairs),
            dma(pairs),
            dma(pairs),
            dma(pairs),
            dma(pairs),
            dma(pairs),
            dma((2,)),
        ],
        compiler_params=pltpu.CompilerParams(
            collective_id=0, has_side_effects=True, vmem_limit_bytes=46 * 2**20
        ),
        name="block_backward",
    )(
        *(
            pltpu.with_memory_space_constraint(arg, pltpu.HBM)
            for arg in (queries, keys, values, out_grad, norm_gain)
        )
    )


def solution(mesh):
    return jax.shard_map(
        shards,
        mesh=mesh,
        in_specs=(
            P("seq", "head"),
            P("seq", "head"),
            P("seq", "head"),
            P("seq", "head"),
            P("head"),
        ),
        out_specs=(P("seq", "head"), P("seq", "head"), P("seq", "head")),
        check_vma=False,
    )
```

time: 714 us -> 67.7 us (0.09)
  waiting for transfers between devices: 544 us -> 0 us
  other arithmetic: 100 us -> 0 us
  Pallas kernels: 0 us -> 64.1 us
  local copies, waits for them, and re-layouts: 22.9 us -> 2.91 us
  matrix products: 19.8 us -> 0 us
  between operations: 14.3 us -> 0.64 us
  blocking collectives: 8.39 us -> 0 us
    all_gather x2 -> x0, waiting for transfers between devices: 544 us -> none  [carried_in(): gathered = lax.all_gather(part, axis)]
    add x63 -> x0, other arithmetic: 93.8 us -> none  [add_terms(): return earlier + later]
    pallas_call x0 -> x1, Pallas kernels: none -> 64.1 us  [shards(): pl.pallas_call(kernel, out_shape=(grad, grad, grad), in_specs=[hbm, hbm,...]
    dot_general x12 -> x0, matrix products: 19.8 us -> none  [the longest x1 3.54 us: shards(): jnp.einsum('hnck,hnce->hnke', masked, delta, preferred_element_type=f32)]
    unnamed x40 -> x3, local copies, waits for them, and re-layouts: 14.7 us -> 2.91 us
    psum x1 -> x0, blocking collectives: 8.39 us -> none  [shards(): square_sum, cross_sum = lax.psum((square_part, cross_part), 'head')]
  transfers between devices with their start and end apart: 2 -> 0, of which waited for: 2 -> 0; matrix products, arithmetic and copies ran while one was open for 2% -> 0% of each run, Pallas kernels for 0% -> 0%
where the time goes in v2:
time: 67.7 us; the launch traced here: 67.6 us
  Pallas kernels  64.1 us (95%)
  local copies, waits for them, and re-layouts  2.91 us (4%)
    pallas_call x1, Pallas kernels, shards(): pl.pallas_call(kernel, out_shape=(grad, grad, grad), in_specs=[hbm, hbm,...  64.1 us
    unnamed x3, local copies, waits for them, and re-layouts  2.91 us

profile of v2, /device:TPU:1, one launch (start us, length us, event | category | flops | bytes accessed | tf_op | source)
XLA Modules:
  0.0 67.6 jit_solution(6572036126739613632)
XLA Ops:
  0.6 64.1 %block_backward.1 = (bf16[256,2048]{1,0:T(8,128)(2,1)S(1)}, bf16[256,2048]{1,0:T(8,128)(2,1)S(1)}, bf16[256,2048]{1,0:T(8,128)(2,1)S(1)}) custom-call(bf16[256,2048]{1,0:T(8,128)(2,1)} %q_hbm.1, bf16[256,2048]{1,0:T(8,128)(2,1)} %k_hbm.1, bf16[256,2048]{1,0:T(8,128)(2,1)} %v_hbm.1, bf16[256,2048]{1,0:T(8,128)(2,1)} %g_hbm.1, bf16[2048]{0:T(1024)(128)(2,1)} %gain_hbm.1), custom_call_target="tpu_custom_call" | custom-call | tf_op jit(solution)/shard_map/block_backward/pallas_call | solution.py:301
  64.7 1.0 %copy.11 = bf16[256,2048]{1,0:T(8,128)(2,1)} copy(bf16[256,2048]{1,0:T(8,128)(2,1)S(1)} %get-tuple-element.6) | data formatting | bytes 2097152
  65.7 1.0 %copy.12 = bf16[256,2048]{1,0:T(8,128)(2,1)} copy(bf16[256,2048]{1,0:T(8,128)(2,1)S(1)} %get-tuple-element.7) | data formatting | bytes 2097152
  66.7 1.0 %copy.13 = bf16[256,2048]{1,0:T(8,128)(2,1)} copy(bf16[256,2048]{1,0:T(8,128)(2,1)S(1)} %get-tuple-element.8) | data formatting | bytes 2097152

commit v3 on v2

--- a/solution.py
+++ b/solution.py
@@ -1,3 +1,5 @@
+import functools
+
 import jax
 import jax.numpy as jnp
 from jax import lax
@@ -19,6 +21,15 @@
 MESH = pl.DeviceIdType.MESH
 FAR_Z = (4, 3, 5, 2, 6, 1, 7)
 FAR_Y = (2, 1, 3)
+FIRST = (
+    "y0", "y1", "y2", "y3", "w", "w", "w", "z0", "z1", "z2", "z3", "w", "w", "r0", "r1", "r2",
+    "r3", "w", "b0", "b1", "b2", "b3", "c0", "c1", "t0", "c2", "t1", "c3", "t2", "t3",
+)
+SECOND = (
+    "s0", "s1", "y0", "s2", "y1", "s3", "y2", "y3", "w", "w", "z0", "z1", "z2", "z3", "w", "w",
+    "r0", "r1", "r2", "r3", "w", "w", "b0", "b1", "b2", "b3", "w", "w", "c0", "c1", "t0", "c2",
+    "t1", "c3", "t2", "t3",
+)
 PEERS = 1 + len(FAR_Z) + len(FAR_Y) + NX - 1
 
 f32 = jnp.float32
@@ -66,7 +77,7 @@
             ((k_hbm, k), (v_hbm, v), (q_hbm, q), (g_hbm, g), (gain_hbm, gain))
         )
     ]
-    for load in loads:
+    for load in loads[:2]:
         load.start()
 
     barrier = pltpu.get_barrier_semaphore()
@@ -94,9 +105,11 @@
             device_id_type=MESH,
         ).start()
 
-    def swap_out(s, c, term):
+    def fill(s, c, term):
         for j in range(PER):
             own[s, 1 - core, c, pl.ds(j * DH, DH)] = term(theirs + c * PER + j)
+
+    def swap_out(s, c):
         send(own.at[s, 1 - core, c], swap.at[s, c], swap_sem.at[s, c], other)
 
     def y_out(s, c, term):
@@ -162,6 +175,29 @@
             wait_for(y_back.at[s, c, pl.ds(0, NY - 1)], yb_sem.at[s, c, 0])
             wait_for(arrived.at[s, c], ahead_sem.at[s, c, 0])
 
+    def run(order, s, reverse, term, inner, use, local):
+        local = list(local)
+        for step in order:
+            name, c = step[0], int(step[1:] or 0)
+            if name == "s":
+                fill(s, c, term)
+                swap_out(s, c)
+            elif name == "y":
+                y_out(s, c, term)
+            elif name == "z":
+                z_out(s, c)
+            elif name == "r":
+                z_return(s, c, reverse)
+            elif name == "b":
+                y_return(s, c, reverse)
+            elif name == "c":
+                collect(s, c, inner, use)
+            elif name == "t":
+                collect_theirs(s, c, use)
+            else:
+                local.pop(0)()
+        assert not local
+
     def heads(first, count, body):
         def pair(i, carry):
             body(first + 2 * i)
@@ -180,13 +216,13 @@
 
     loads[0].wait()
     loads[1].wait()
+    for c in chunks:
+        fill(0, c, key_value)
+    for load in loads[2:]:
+        load.start()
     pl.semaphore_wait(barrier, PEERS)
     for c in chunks:
-        swap_out(0, c, key_value)
-    for c in chunks:
-        y_out(0, c, key_value)
-    for load in loads[2:]:
-        load.wait()
+        swap_out(0, c)
 
     def within(head):
         at = cols(head)
@@ -202,15 +238,6 @@
         scaled[:, at] = gain[at].astype(f32).reshape(1, 2 * DH) * g[:, at].astype(f32)
         return carry
 
-    heads(0, HALF, within)
-    for c in chunks:
-        z_out(0, c)
-    heads(HALF, HALF, within)
-    for c in chunks:
-        z_return(0, c, False)
-    lax.fori_loop(0, HEADS // 2, prepare, 0)
-    for c in chunks:
-        y_return(0, c, False)
     norm_acc[...] = jnp.zeros_like(norm_acc)
 
     def finish_attn(head, state_b):
@@ -221,10 +248,16 @@
         norm_acc[0] += value * value
         norm_acc[1] += scaled[:, at] * value
 
-    for c in chunks:
-        collect(0, c, 0, finish_attn)
-    for c in chunks:
-        collect_theirs(0, c, finish_attn)
+    def load_rest():
+        for load in loads[2:]:
+            load.wait()
+
+    run(
+        FIRST, 0, False, key_value, 0, finish_attn,
+        [load_rest]
+        + [functools.partial(heads, i, 4, within) for i in range(0, HEADS, 4)]
+        + [lambda: lax.fori_loop(0, HEADS // 2, prepare, 0)],
+    )
 
     norm_got[plane, 0:1] = jnp.sum(norm_acc[0].T, axis=0, keepdims=True)
     norm_got[plane, 1:2] = jnp.sum(norm_acc[1].T, axis=0, keepdims=True)
@@ -235,7 +268,6 @@
     features = float(NX * HEADS * DH)
     inverse = lax.rsqrt(sums[0:1] / features + 1e-05)
     weight = inverse * inverse * inverse * (sums[1:2] / features)
-    wait_for(norm_got.at[pl.ds(0, NX - 1)], norm_sem.at[0])
     norm_acc[0] = jnp.broadcast_to(inverse, (DH, GROUP)).T
     norm_acc[1] = jnp.broadcast_to(weight, (DH, GROUP)).T
 
@@ -244,11 +276,6 @@
         value = (norm_acc[0] * scaled[:, at] - attn[:, at] * norm_acc[1]).astype(bf16)
         delta[:, at] = value
         return dot(q_t[head], value, 1, 0)
-
-    for c in chunks:
-        swap_out(1, c, query_delta)
-    for c in chunks:
-        y_out(1, c, query_delta)
 
     def query_side(head):
         at = cols(head)
@@ -263,28 +290,30 @@
         kg_part[:, at] = dot(dscore[head], q[:, at], 0, 0)
         vg_part[:, at] = dot(scores[head], delta[:, at], 0, 0)
 
-    heads(0, HALF, query_side)
-    for c in chunks:
-        z_out(1, c)
-    heads(HALF, HALF, query_side)
-    for c in chunks:
-        z_return(1, c, True)
-    heads(0, HALF, key_side)
-    for c in chunks:
-        y_return(1, c, True)
-    heads(HALF, HALF, key_side)
-
     def finish_keys(head, later_b):
         at = cols(head)
         kg[:, at] = (kg_part[:, at] + dot(v[:, at], later_b, 1, 1)).astype(bf16)
         vg[:, at] = (vg_part[:, at] + dot(k[:, at], later_b, 1, 0)).astype(bf16)
 
-    for c in chunks:
-        collect(1, c, 1, finish_keys)
-    for c in chunks:
-        collect_theirs(1, c, finish_keys)
+    run(
+        SECOND, 1, True, query_delta, 1, finish_keys,
+        [functools.partial(heads, i, 4, query_side) for i in range(0, HEADS, 4)]
+        + [functools.partial(heads, i, 4, key_side) for i in range(0, HEADS, 4)],
+    )
+    wait_for(norm_got.at[pl.ds(0, NX - 1)], norm_sem.at[0])
     finish_sends(0)
     finish_sends(1)
+
+
+def write_out(a, b, c, a_out, b_out, c_out, sem):
+    copies = [
+        pltpu.make_async_copy(src, dst, sem.at[i])
+        for i, (src, dst) in enumerate(((a, a_out), (b, b_out), (c, c_out)))
+    ]
+    for copy in copies:
+        copy.start()
+    for copy in copies:
+        copy.wait()
 
 
 def shards(queries, keys, values, out_grad, norm_gain):
@@ -298,7 +327,7 @@
     by_y = (2, CHUNKS, NY, YROWS, DH)
     by_z = (2, CHUNKS, NZ, ZROWS, DH)
     pairs = (2, CHUNKS, 2)
-    return pl.pallas_call(
+    results = pl.pallas_call(
         kernel,
         out_shape=(grad, grad, grad),
         in_specs=[hbm, hbm, hbm, hbm, hbm],
@@ -351,6 +380,15 @@
             for arg in (queries, keys, values, out_grad, norm_gain)
         )
     )
+    return pl.pallas_call(
+        write_out,
+        out_shape=(grad, grad, grad),
+        in_specs=[on_chip, on_chip, on_chip],
+        out_specs=(hbm, hbm, hbm),
+        scratch_shapes=[dma((3,))],
+        compiler_params=pltpu.CompilerParams(vmem_limit_bytes=4 * 2**20),
+        name="stage_out",
+    )(*results)
 
 
 def solution(mesh):

time: 67.7 us -> 66.8 us (0.987)
  local copies, waits for them, and re-layouts: 2.91 us -> 0 us
  Pallas kernels: 64.1 us -> 66 us
    unnamed x3 -> x0, local copies, waits for them, and re-layouts: 2.91 us -> none
    pallas_call x0 -> x1, Pallas kernels: none -> 1.69 us  [shards(): pl.pallas_call(write_out, out_shape=(grad, grad, grad), in_specs=[on_chip...]
where the time goes in v3:
time: 66.8 us; the launch traced here: 66.7 us
  Pallas kernels  66 us (99%)
    pallas_call x1, Pallas kernels, shards(): pl.pallas_call(kernel, out_shape=(grad, grad, grad), in_specs=[hbm, hbm,...  64.3 us
    pallas_call x1, Pallas kernels, shards(): pl.pallas_call(write_out, out_shape=(grad, grad, grad), in_specs=[on_chip...  1.69 us

profile of v3, /device:TPU:1, one launch (start us, length us, event | category | flops | bytes accessed | tf_op | source)
XLA Modules:
  0.0 66.7 jit_solution(12356333128862313610)
XLA Ops:
  0.6 64.3 %block_backward.1 = (bf16[256,2048]{1,0:T(8,128)(2,1)S(1)}, bf16[256,2048]{1,0:T(8,128)(2,1)S(1)}, bf16[256,2048]{1,0:T(8,128)(2,1)S(1)}) custom-call(bf16[256,2048]{1,0:T(8,128)(2,1)} %q_hbm.1, bf16[256,2048]{1,0:T(8,128)(2,1)} %k_hbm.1, bf16[256,2048]{1,0:T(8,128)(2,1)} %v_hbm.1, bf16[256,2048]{1,0:T(8,128)(2,1)} %g_hbm.1, bf16[2048]{0:T(1024)(128)(2,1)} %gain_hbm.1), custom_call_target="tpu_custom_call" | custom-call | tf_op jit(solution)/shard_map/block_backward/pallas_call | solution.py:330
  65.0 1.7 %stage_out.1 = (bf16[256,2048]{1,0:T(8,128)(2,1)}, bf16[256,2048]{1,0:T(8,128)(2,1)}, bf16[256,2048]{1,0:T(8,128)(2,1)}) custom-call(bf16[256,2048]{1,0:T(8,128)(2,1)S(1)} %get-tuple-element.6.a, bf16[256,2048]{1,0:T(8,128)(2,1)S(1)} %get-tuple-element.7.b, bf16[256,2048]{1,0:T(8,128)(2,1)S(1)} %get-tuple-element.8.c), custom_call_target="tpu_custom_call" | custom-call | tf_op jit(solution)/shard_map/stage_out/pallas_call | solution.py:383

commit v4 on v3

--- a/solution.py
+++ b/solution.py
@@ -22,12 +22,12 @@
 FAR_Z = (4, 3, 5, 2, 6, 1, 7)
 FAR_Y = (2, 1, 3)
 FIRST = (
-    "y0", "y1", "y2", "y3", "w", "w", "w", "z0", "z1", "z2", "z3", "w", "w", "r0", "r1", "r2",
-    "r3", "w", "b0", "b1", "b2", "b3", "c0", "c1", "t0", "c2", "t1", "c3", "t2", "t3",
+    "y0", "y1", "y2", "y3", "w", "w", "w", "z0", "z1", "z2", "r0", "z3", "w", "w", "r1", "r2", "b0",
+    "r3", "w", "b1", "b2", "b3", "c0", "c1", "t0", "c2", "t1", "c3", "t2", "t3",
 )
 SECOND = (
-    "s0", "s1", "y0", "s2", "y1", "s3", "y2", "y3", "w", "w", "z0", "z1", "z2", "z3", "w", "w",
-    "r0", "r1", "r2", "r3", "w", "w", "b0", "b1", "b2", "b3", "w", "w", "c0", "c1", "t0", "c2",
+    "s0", "s1", "y0", "s2", "y1", "s3", "y2", "y3", "w", "w", "z0", "z1", "z2", "r0", "z3", "w", "w",
+    "r1", "r2", "b0", "r3", "w", "w", "b1", "b2", "b3", "w", "w", "c0", "c1", "t0", "c2",
     "t1", "c3", "t2", "t3",
 )
 PEERS = 1 + len(FAR_Z) + len(FAR_Y) + NX - 1

time: 66.8 us -> 66.3 us (level)
  no operation moved by 1% of the time
where the time goes in v4:
time: 66.3 us; the launch traced here: 66.2 us
  Pallas kernels  65.6 us (99%)
    pallas_call x1, Pallas kernels, shards(): pl.pallas_call(kernel, out_shape=(grad, grad, grad), in_specs=[hbm, hbm,...  63.9 us
    pallas_call x1, Pallas kernels, shards(): pl.pallas_call(write_out, out_shape=(grad, grad, grad), in_specs=[on_chip...  1.69 us

profile of v4, /device:TPU:1, one launch (start us, length us, event | category | flops | bytes accessed | tf_op | source)
XLA Modules:
  0.0 66.2 jit_solution(5562876110322007339)
XLA Ops:
  0.6 63.9 %block_backward.1 = (bf16[256,2048]{1,0:T(8,128)(2,1)S(1)}, bf16[256,2048]{1,0:T(8,128)(2,1)S(1)}, bf16[256,2048]{1,0:T(8,128)(2,1)S(1)}) custom-call(bf16[256,2048]{1,0:T(8,128)(2,1)} %q_hbm.1, bf16[256,2048]{1,0:T(8,128)(2,1)} %k_hbm.1, bf16[256,2048]{1,0:T(8,128)(2,1)} %v_hbm.1, bf16[256,2048]{1,0:T(8,128)(2,1)} %g_hbm.1, bf16[2048]{0:T(1024)(128)(2,1)} %gain_hbm.1), custom_call_target="tpu_custom_call" | custom-call | tf_op jit(solution)/shard_map/block_backward/pallas_call | solution.py:330
  64.5 1.7 %stage_out.1 = (bf16[256,2048]{1,0:T(8,128)(2,1)}, bf16[256,2048]{1,0:T(8,128)(2,1)}, bf16[256,2048]{1,0:T(8,128)(2,1)}) custom-call(bf16[256,2048]{1,0:T(8,128)(2,1)S(1)} %get-tuple-element.6.a, bf16[256,2048]{1,0:T(8,128)(2,1)S(1)} %get-tuple-element.7.b, bf16[256,2048]{1,0:T(8,128)(2,1)S(1)} %get-tuple-element.8.c), custom_call_target="tpu_custom_call" | custom-call | tf_op jit(solution)/shard_map/stage_out/pallas_call | solution.py:383

commit v5 on v4

--- a/solution.py
+++ b/solution.py
@@ -22,12 +22,12 @@
 FAR_Z = (4, 3, 5, 2, 6, 1, 7)
 FAR_Y = (2, 1, 3)
 FIRST = (
-    "y0", "y1", "y2", "y3", "w", "w", "w", "z0", "z1", "z2", "r0", "z3", "w", "w", "r1", "r2", "b0",
-    "r3", "w", "b1", "b2", "b3", "c0", "c1", "t0", "c2", "t1", "c3", "t2", "t3",
+    "y0", "y1", "y2", "y3", "w", "z0", "w", "z1", "w", "z2", "r0", "z3", "w", "r1", "w", "r2",
+    "b0", "r3", "w", "b1", "b2", "b3", "c0", "c1", "t0", "c2", "t1", "c3", "t2", "t3",
 )
 SECOND = (
-    "s0", "s1", "y0", "s2", "y1", "s3", "y2", "y3", "w", "w", "z0", "z1", "z2", "r0", "z3", "w", "w",
-    "r1", "r2", "b0", "r3", "w", "w", "b1", "b2", "b3", "w", "w", "c0", "c1", "t0", "c2",
+    "s0", "s1", "y0", "s2", "y1", "s3", "y2", "y3", "w", "z0", "w", "z1", "w", "z2", "r0", "z3",
+    "w", "r1", "w", "r2", "b0", "r3", "w", "b1", "w", "b2", "b3", "w", "c0", "c1", "t0", "c2",
     "t1", "c3", "t2", "t3",
 )
 PEERS = 1 + len(FAR_Z) + len(FAR_Y) + NX - 1

time: 66.3 us -> 66.2 us (level)
  no operation moved by 1% of the time
where the time goes in v5:
time: 66.2 us; the launch traced here: 66.1 us
  Pallas kernels  65.4 us (99%)
    pallas_call x1, Pallas kernels, shards(): pl.pallas_call(kernel, out_shape=(grad, grad, grad), in_specs=[hbm, hbm,...  63.8 us
    pallas_call x1, Pallas kernels, shards(): pl.pallas_call(write_out, out_shape=(grad, grad, grad), in_specs=[on_chip...  1.69 us

profile of v5, /device:TPU:1, one launch (start us, length us, event | category | flops | bytes accessed | tf_op | source)
XLA Modules:
  0.0 66.1 jit_solution(7620157989384953961)
XLA Ops:
  0.6 63.8 %block_backward.1 = (bf16[256,2048]{1,0:T(8,128)(2,1)S(1)}, bf16[256,2048]{1,0:T(8,128)(2,1)S(1)}, bf16[256,2048]{1,0:T(8,128)(2,1)S(1)}) custom-call(bf16[256,2048]{1,0:T(8,128)(2,1)} %q_hbm.1, bf16[256,2048]{1,0:T(8,128)(2,1)} %k_hbm.1, bf16[256,2048]{1,0:T(8,128)(2,1)} %v_hbm.1, bf16[256,2048]{1,0:T(8,128)(2,1)} %g_hbm.1, bf16[2048]{0:T(1024)(128)(2,1)} %gain_hbm.1), custom_call_target="tpu_custom_call" | custom-call | tf_op jit(solution)/shard_map/block_backward/pallas_call | solution.py:330
  64.4 1.7 %stage_out.1 = (bf16[256,2048]{1,0:T(8,128)(2,1)}, bf16[256,2048]{1,0:T(8,128)(2,1)}, bf16[256,2048]{1,0:T(8,128)(2,1)}) custom-call(bf16[256,2048]{1,0:T(8,128)(2,1)S(1)} %get-tuple-element.6.a, bf16[256,2048]{1,0:T(8,128)(2,1)S(1)} %get-tuple-element.7.b, bf16[256,2048]{1,0:T(8,128)(2,1)S(1)} %get-tuple-element.8.c), custom_call_target="tpu_custom_call" | custom-call | tf_op jit(solution)/shard_map/stage_out/pallas_call | solution.py:383
